TPU v7x, 32 devices: a whole 2x2x4 slice. The times are simulated.
32 devices in a mesh: grp: 2 (over x), lat: 8 (over z, y), lon: 2 (over core).
Axes of the slice: x: 2, y: 2, z: 4, core: 2. Of those that a mesh axis runs over, the one named last changes fastest.
Arguments:
- perturb: float32 [256, 256, 192], P(('grp', 'lat'), 'lon'), parts along dimension 0, may hold values from -110 to 110, as said below
- kernels: float32 [2, 7, 7, 192], replicated, may hold values from -0.875 to 0.875
- gains: float32 [2, 192], replicated, may hold values from 0.5 to 1.5
- w_in: bfloat16 [2, 192, 768], replicated, may hold values from -0.4375 to 0.4375
- w_out: bfloat16 [2, 768, 192], replicated, may hold values from -0.21875 to 0.21875
- scales: float32 [2, 192], replicated, may hold values from 0.3 to 1.5
- normed: bfloat16 [2, 256, 256, 192], P(None, ('grp', 'lat'), 'lon'), parts along dimension 1, may hold values from -6 to 6
- inv_std: float32 [2, 256, 256], P(None, ('grp', 'lat'), 'lon'), parts along dimension 1, may hold values from 0.5 to 2
- slope: bfloat16 [2, 256, 256, 768], P(None, ('grp', 'lat'), 'lon'), parts along dimension 1, may hold values from -0.099609375 to 1.09375
Outputs:
- new_vec: float32 [256, 256, 192], P(('grp', 'lat'), 'lon'), parts along dimension 0
- growth: float32 [2], P('grp'), parts along dimension 0
There are 2 independent parts, one for each index of `grp`. A program takes and returns all parts, laid end to end along the dimension named above; an argument that names none is the same for every part. Nothing has to cross between parts.
Inputs may be any that keep to these rules, and one draw needn't show every extreme that they name: `perturb`: the initial perturbation.
All inputs are finite; a program needn't handle non-finite values.
Results may differ from a plain program's by a relative error of at most 0.0075.
Values may be sent and summed in bfloat16 or wider, within the bound.
No kernel may reach another device: no remote copies, remote signals or barrier semaphores. Data moves between devices by JAX's collectives and lax.ppermute only.
A program may use at most 64 MiB of HBM per device.

v0:
```python
import math
import jax
import jax.numpy as jnp
from jax import lax
from jax.sharding import PartitionSpec as P

lat_span = 70.0 * math.pi / 180.0


def extended(x, sides, width, wrap):
    for axis, dim in sides:
        size, length = (lax.axis_size(axis), x.shape[dim])
        up = [(i, (i + 1) % size) for i in range(size if wrap else size - 1)]
        down = [(j, i) for i, j in up]
        last = lax.slice_in_dim(x, length - width, length, axis=dim)
        initial = lax.slice_in_dim(x, 0, width, axis=dim)
        before = lax.ppermute(last, axis, up)
        after = lax.ppermute(initial, axis, down)
        x = jnp.concatenate([before, x, after], axis=dim)
    return x


def tangent_pad(rounded):
    widened = extended(rounded, (("lon", 1),), 3, True)
    return extended(widened, (("lat", 0),), 3, False)


def adjoint_pad(rounded):
    widened = extended(rounded, (("lon", 1),), 3, True)
    return extended(widened, (("lat", 0),), 3, False)


def window_sum(padded, kernel, row_count, col_count, flipped):
    summed = jnp.zeros((row_count, col_count, padded.shape[2]), jnp.float32)
    for row_off in range(7):
        for col_off in range(7):
            row_start = 6 - row_off if flipped else row_off
            col_start = 6 - col_off if flipped else col_off
            window_part = padded[
                row_start : row_start + row_count, col_start : col_start + col_count
            ].astype(jnp.float32)
            summed = summed + kernel[row_off, col_off] * window_part
    return summed


def project(values, normed_layer, inv_layer):
    normal_f = normed_layer.astype(jnp.float32)
    centred = (
        values
        - jnp.mean(values, axis=-1, keepdims=True)
        - normal_f * jnp.mean(normal_f * values, axis=-1, keepdims=True)
    )
    return inv_layer[..., None] * centred


def on_device(perturb, kernels, gains, w_in, w_out, scales, normed, inv_std, slope):
    row_count, col_count, chans = perturb.shape
    lat_total = row_count * lax.axis_size("lat")
    lon_total = col_count * lax.axis_size("lon")
    local_rows = (lax.axis_index("lat") * row_count + jnp.arange(row_count)).astype(jnp.float32)
    area_rows = jnp.cos(lat_span * (local_rows + 0.5) / lat_total)
    area_w = area_rows[:, None, None]
    every_row = jnp.arange(lat_total).astype(jnp.float32)
    weight_total = jnp.sum(jnp.cos(lat_span * (every_row + 0.5) / lat_total)) * lon_total * chans
    layer_count = kernels.shape[0]
    tangent = perturb
    for layer_index in range(layer_count):
        rounded = tangent.astype(jnp.bfloat16)
        padded = tangent_pad(rounded)
        conv_out = window_sum(padded, kernels[layer_index], row_count, col_count, False)
        tangent_norm = project(conv_out, normed[layer_index], inv_std[layer_index])
        operand = (gains[layer_index] * tangent_norm).astype(jnp.bfloat16)
        hidden_pre = jnp.dot(operand, w_in[layer_index], preferred_element_type=jnp.float32)
        gated = (slope[layer_index] * hidden_pre).astype(jnp.bfloat16)
        branch_out = jnp.dot(gated, w_out[layer_index], preferred_element_type=jnp.float32)
        tangent = tangent + scales[layer_index] * branch_out
    start_local = jnp.sum(area_w * perturb * perturb)
    forward_local = jnp.sum(area_w * tangent * tangent)
    grad_field = area_w * tangent
    for layer_index in range(layer_count - 1, -1, -1):
        scaled = (scales[layer_index] * grad_field).astype(jnp.bfloat16)
        hidden_back = lax.dot_general(
            scaled, w_out[layer_index], (((2,), (1,)), ((), ())), preferred_element_type=jnp.float32
        )
        gated = (slope[layer_index] * hidden_back).astype(jnp.bfloat16)
        chan_back = lax.dot_general(
            gated, w_in[layer_index], (((2,), (1,)), ((), ())), preferred_element_type=jnp.float32
        )
        conv_grad = project(
            gains[layer_index] * chan_back, normed[layer_index], inv_std[layer_index]
        ).astype(jnp.bfloat16)
        padded = adjoint_pad(conv_grad)
        conv_back = window_sum(padded, kernels[layer_index], row_count, col_count, True)
        grad_field = grad_field + conv_back
    adjoint_out = grad_field / area_w
    adjoint_local = jnp.sum(area_w * adjoint_out * adjoint_out)
    start_sum, forward_sum, adjoint_sum = lax.psum(
        (start_local, forward_local, adjoint_local), ("lat", "lon")
    )
    start_sq = start_sum / weight_total
    forward_sq = forward_sum / weight_total
    adjoint_sq = adjoint_sum / weight_total
    growth = jnp.sqrt(forward_sq / (start_sq + 1e-06)).reshape(1)
    new_vec = adjoint_out / jnp.sqrt(adjoint_sq + 1e-06)
    return (new_vec, growth)


def solution(mesh):
    in_specs = (
        P(("grp", "lat"), "lon", None),
        P(),
        P(),
        P(),
        P(),
        P(),
        P(None, ("grp", "lat"), "lon", None),
        P(None, ("grp", "lat"), "lon"),
        P(None, ("grp", "lat"), "lon", None),
    )
    out_specs = (P(("grp", "lat"), "lon", None), P("grp"))
    return jax.shard_map(
        on_device, mesh=mesh, in_specs=in_specs, out_specs=out_specs, check_vma=False
    )
```

profile of v0, /device:TPU:0, one launch (start us, length us, event | category | flops | bytes accessed | tf_op | source)
XLA Modules:
  0.0 238.3 jit_solution(1238597391319515903)
XLA Ops:
  7.7 4.9 %collective-permute-start.2 = (bf16[3,134,192]{1,2,0:T(8,128)(2,1)S(1)}, bf16[3,134,192]{1,2,0:T(8,128)(2,1)S(1)}, u32[]{:S(2)}, u32[]{:S(2)}) collective-permute-start(bf16[3,134,192]{1,2,0:T(8,128)(2,1)S(1)} %get-tuple-element.33), channel_id=1, source_target_pairs={{0,2},{2,4},{4,6},{6,8},{8,10},{10,12},{12,14},{1,3},{3,5},{5,7},{... | collective-permute-start | bytes 463112 | tf_op jit(solution)/shard_map/ppermute | solution.py:17
  14.5 10.8 %collective-permute-done.2 = bf16[3,134,192]{1,2,0:T(8,128)(2,1)S(1)} collective-permute-done((bf16[3,134,192]{1,2,0:T(8,128)(2,1)S(1)}, bf16[3,134,192]{1,2,0:T(8,128)(2,1)S(1)}, u32[]{:S(2)}, u32[]{:S(2)}) %collective-permute-start.2) | collective-permute-done | bytes 154400 | tf_op jit(solution)/shard_map/ppermute | solution.py:17
  25.3 2.2 maximum_maximum_fusion
  28.0 18.3 %fusion.139 = (f32[16,128]{1,0:T(8,128)S(1)}, f32[16,128]{1,0:T(8,128)S(1)}, f32[16,128,192]{1,2,0:T(8,128)}) fusion(bf16[2,16,128,192]{2,3,1,0:T(8,128)(2,1)S(1)} %copy-done.5, bf16[19,134,192]{1,2,0:T(8,128)(2,1)S(1)} %get-tuple-element.32, f32[192]{0:T(256)S(1)} %bitcast.247, f32[192]{0:T(256)S(1)} %bitcast.249, f32[192]{0:T(256)S(1)} %bitcast.251, ...), kind=kLoop, calls=%fused_computation.193 | loop fusion | flops 66056192 | bytes 36266752 | tf_op jit(solution)/shard_map/reduce_sum | solution.py:50
  46.3 6.5 %fusion.153 = (bf16[16,128,192]{1,2,0:T(8,128)(2,1)S(1)}, f32[16,128,192]{1,2,0:T(8,128)}) fusion(f32[16,128,192]{1,2,0:T(8,128)} %param.9, bf16[2,768,192]{1,2,0:T(8,128)(2,1)S(1)} %copy-done.170, bf16[2,16,128,768]{3,2,1,0:T(8,128)(2,1)} %param.17, f32[16,128,192]{1,2,0:T(8,128)} %get-tuple-element.18, f32[16,128]{1,0:T(8,128)S(1)} %broadcast_multiply_fusion.6, ...), kind=kOutput, calls=%fused_computation.207 | convolution fusion | flops 1216610304 | bytes 10053632 | tf_op jit(solution)/shard_map/dot_general | solution.py:75
  56.4 4.4 %collective-permute-start.6 = (bf16[3,134,192]{1,2,0:T(8,128)(2,1)S(1)}, bf16[3,134,192]{1,2,0:T(8,128)(2,1)S(1)}, u32[]{:S(2)}, u32[]{:S(2)}) collective-permute-start(bf16[3,134,192]{1,2,0:T(8,128)(2,1)S(1)} %get-tuple-element.29), channel_id=1, source_target_pairs={{0,2},{2,4},{4,6},{6,8},{8,10},{10,12},{12,14},{1,3},{3,5},{5,7},{... | collective-permute-start | bytes 463112 | tf_op jit(solution)/shard_map/ppermute | solution.py:17
  64.8 8.8 %collective-permute-done.6 = bf16[3,134,192]{1,2,0:T(8,128)(2,1)S(1)} collective-permute-done((bf16[3,134,192]{1,2,0:T(8,128)(2,1)S(1)}, bf16[3,134,192]{1,2,0:T(8,128)(2,1)S(1)}, u32[]{:S(2)}, u32[]{:S(2)}) %collective-permute-start.6) | collective-permute-done | bytes 154400 | tf_op jit(solution)/shard_map/ppermute | solution.py:17
  73.6 2.2 maximum_maximum_fusion.1
  76.3 18.0 %fusion.138 = (f32[16,128]{1,0:T(8,128)S(1)}, f32[16,128]{1,0:T(8,128)S(1)}, f32[16,128,192]{1,2,0:T(8,128)}) fusion(bf16[2,16,128,192]{2,3,1,0:T(8,128)(2,1)S(1)} %copy-done.6, bf16[19,134,192]{1,2,0:T(8,128)(2,1)S(1)} %get-tuple-element.28, f32[192]{0:T(256)S(1)} %bitcast.285, f32[192]{0:T(256)S(1)} %bitcast.287, f32[192]{0:T(256)S(1)} %bitcast.289, ...), kind=kLoop, calls=%fused_computation.192 | loop fusion | flops 66056192 | bytes 36266752 | tf_op jit(solution)/shard_map/reduce_sum | solution.py:50
  94.4 5.4 %multiply_add_fusion.1 = f32[16,128,192]{1,2,0:T(8,128)S(1)} fusion(f32[16,128,192]{1,2,0:T(8,128)} %get-tuple-element.150, bf16[2,16,128,768]{3,2,1,0:T(8,128)(2,1)} %param.17, f32[16,128,192]{1,2,0:T(8,128)} %get-tuple-element.17, f32[16,128]{1,0:T(8,128)S(1)} %broadcast_multiply_fusion.4, f32[16,128]{1,0:T(8,128)S(1)} %broadcast_multiply_fusion.5, ...), kind=kOutput, calls=%fused_computation.101 | convolution fusion | flops 1216217088 | bytes 9267200 | tf_op jit(solution)/shard_map/dot_general | solution.py:75
  99.9 6.0 %fusion.137 = (f32[16,128]{1,0:T(8,128)S(1)}, f32[16,128]{1,0:T(8,128)S(1)}, f32[16,128,192]{1,2,0:T(8,128)}) fusion(bf16[2,16,128,192]{2,3,1,0:T(8,128)(2,1)S(1)} %copy-done.7, bf16[2,192,768]{2,1,0:T(8,128)(2,1)} %param.12, bf16[2,16,128,768]{3,2,1,0:T(8,128)(2,1)} %param.17, f32[16,128,192]{1,2,0:T(8,128)S(1)} %multiply_add_fusion.1, ...), kind=kOutput, calls=%fused_computation.191 | convolution fusion | flops 1215819776 | bytes 7685696 | tf_op jit(solution)/shard_map/dot_general | solution.py:86
  112.7 5.4 %collective-permute-start.11 = (bf16[3,134,192]{1,2,0:T(8,128)(2,1)S(1)}, bf16[3,134,192]{1,2,0:T(8,128)(2,1)S(1)}, u32[]{:S(2)}, u32[]{:S(2)}) collective-permute-start(bf16[3,134,192]{1,2,0:T(8,128)(2,1)S(1)} %get-tuple-element.26), channel_id=1, source_target_pairs={{0,2},{2,4},{4,6},{6,8},{8,10},{10,12},{12,14},{1,3},{3,5},{5,7},{... | collective-permute-start | bytes 463112 | tf_op jit(solution)/shard_map/ppermute | solution.py:17
  118.1 4.8 %collective-permute-done.10 = bf16[3,134,192]{1,2,0:T(8,128)(2,1)S(1)} collective-permute-done((bf16[3,134,192]{1,2,0:T(8,128)(2,1)S(1)}, bf16[3,134,192]{1,2,0:T(8,128)(2,1)S(1)}, u32[]{:S(2)}, u32[]{:S(2)}) %collective-permute-start.10) | collective-permute-done | bytes 154400 | tf_op jit(solution)/shard_map/ppermute | solution.py:18
  122.9 7.2 %collective-permute-done.11 = bf16[3,134,192]{1,2,0:T(8,128)(2,1)S(1)} collective-permute-done((bf16[3,134,192]{1,2,0:T(8,128)(2,1)S(1)}, bf16[3,134,192]{1,2,0:T(8,128)(2,1)S(1)}, u32[]{:S(2)}, u32[]{:S(2)}) %collective-permute-start.11) | collective-permute-done | bytes 154400 | tf_op jit(solution)/shard_map/ppermute | solution.py:17
  130.1 2.2 pad_maximum_fusion.2
  132.7 17.1 %multiply_add_fusion = f32[16,128,192]{1,2,0:T(8,128)} fusion(f32[16,128,192]{1,2,0:T(8,128)S(1)} %copy-done.1, bf16[16,128,192]{1,2,0:T(8,128)(2,1)S(1)} %fusion.49, bf16[16,3,192]{1,2,0:T(8,128)(2,1)S(1)} %copy.29, bf16[16,3,192]{1,2,0:T(8,128)(2,1)S(1)} %copy.30, bf16[19,134,192]{1,2,0:T(8,128)(2,1)S(1)} %get-tuple-element.24, ...), kind=kLoop, calls=%fused_computation.35 | loop fusion | flops 65273856 | bytes 37036864 | tf_op jit(solution)/shard_map/add | solution.py:94
  149.8 6.2 %fusion.136 = (f32[16,128]{1,0:T(8,128)S(1)}, f32[16,128]{1,0:T(8,128)S(1)}, f32[16,128,192]{1,2,0:T(8,128)}) fusion(bf16[2,16,128,192]{2,3,1,0:T(8,128)(2,1)} %param.15, bf16[2,192,768]{2,1,0:T(8,128)(2,1)} %param.12, bf16[2,16,128,768]{3,2,1,0:T(8,128)(2,1)} %param.17, f32[16,128,192]{1,2,0:T(8,128)} %multiply_add_fusion, f32[192]{0:T(256)} %bitcast, ...), kind=kOutput, calls=%fused_computation.190 | convolution fusion | flops 1215426560 | bytes 7686144 | tf_op jit(solution)/shard_map/dot_general | solution.py:86
  162.4 5.3 %collective-permute-start.15 = (bf16[3,134,192]{1,2,0:T(8,128)(2,1)S(1)}, bf16[3,134,192]{1,2,0:T(8,128)(2,1)S(1)}, u32[]{:S(2)}, u32[]{:S(2)}) collective-permute-start(bf16[3,134,192]{1,2,0:T(8,128)(2,1)S(1)} %get-tuple-element.22), channel_id=1, source_target_pairs={{0,2},{2,4},{4,6},{6,8},{8,10},{10,12},{12,14},{1,3},{3,5},{5,7},{... | collective-permute-start | bytes 463112 | tf_op jit(solution)/shard_map/ppermute | solution.py:17
  169.4 3.6 %collective-permute-done.14 = bf16[3,134,192]{1,2,0:T(8,128)(2,1)S(1)} collective-permute-done((bf16[3,134,192]{1,2,0:T(8,128)(2,1)S(1)}, bf16[3,134,192]{1,2,0:T(8,128)(2,1)S(1)}, u32[]{:S(2)}, u32[]{:S(2)}) %collective-permute-start.14) | collective-permute-done | bytes 154400 | tf_op jit(solution)/shard_map/ppermute | solution.py:18
  173.0 6.5 %collective-permute-done.15 = bf16[3,134,192]{1,2,0:T(8,128)(2,1)S(1)} collective-permute-done((bf16[3,134,192]{1,2,0:T(8,128)(2,1)S(1)}, bf16[3,134,192]{1,2,0:T(8,128)(2,1)S(1)}, u32[]{:S(2)}, u32[]{:S(2)}) %collective-permute-start.15) | collective-permute-done | bytes 154400 | tf_op jit(solution)/shard_map/ppermute | solution.py:17
  179.5 2.2 pad_maximum_fusion.3
  182.1 18.2 %fusion.31 = (f32[]{:T(128)}, f32[]{:T(128)}, f32[]{:T(128)}, f32[16,128,192]{1,2,0:T(8,128)}) fusion(f32[16,128,192]{1,2,0:T(8,128)S(1)} %copy-done.4, f32[16]{0:T(128)} %multiply_cosine_fusion, f32[16,128,192]{1,2,0:T(8,128)S(1)} %copy-done.2, f32[16,128,192]{1,2,0:T(8,128)S(1)} %copy-done.3, bf16[19,134,192]{1,2,0:T(8,128)(2,1)S(1)} %get-tuple-element.20, ...), kind=kLoop, calls=%fused_computation.80 | loop fusion | flops 68812800 | bytes 40182604 | tf_op jit(solution)/shard_map/reduce_sum | solution.py:77
  200.3 32.1 %all-reduce = (f32[]{:T(128)}, f32[]{:T(128)}, f32[]{:T(128)}) all-reduce(f32[]{:T(128)} %get-tuple-element.11, f32[]{:T(128)} %get-tuple-element.12, f32[]{:T(128)} %get-tuple-element.10), channel_id=1, replica_groups=mesh['grp'=2,'lat'=8,'lon'=2] {'lat','lon'}, use_global_device_ids=true, to_apply=%region_9.0 | all-reduce | flops 3 | bytes 24 | tf_op jit(solution)/shard_map/psum | solution.py:97
  234.4 2.8 %broadcast_divide_fusion = f32[16,128,192]{1,2,0:T(8,128)} fusion(f32[16,128,192]{1,2,0:T(8,128)} %get-tuple-element.16, f32[16]{0:T(128)S(1)} %broadcast_multiply_fusion.8), kind=kLoop, calls=%fused_computation.133 | loop fusion | flops 393216 | bytes 3145792 | tf_op jit(solution)/shard_map/div | solution.py:104
  (413 shorter events, 29.9 us)
Async XLA Ops:
  2.9 3.5 %collective-permute-start = (bf16[16,3,192]{2,0,1:T(8,128)(2,1)S(1)}, bf16[16,3,192]{2,0,1:T(8,128)(2,1)S(1)}, u32[]{:S(2)}, u32[]{:S(2)}) collective-permute-start(bf16[16,3,192]{2,0,1:T(8,128)(2,1)S(1)} %copy.14), channel_id=1, source_target_pairs={{0,1},{1,0},{2,3},{3,2},{4,5},{5,4},{6,7},{7,6},{8,9},{9,8},{10,11... | collective-permute-start | bytes 55304 | tf_op jit(solution)/shard_map/ppermute | solution.py:17
  3.8 3.0 %collective-permute-start.1 = (bf16[16,3,192]{2,0,1:T(8,128)(2,1)S(1)}, bf16[16,3,192]{2,0,1:T(8,128)(2,1)S(1)}, u32[]{:S(2)}, u32[]{:S(2)}) collective-permute-start(bf16[16,3,192]{2,0,1:T(8,128)(2,1)S(1)} %copy.15), channel_id=1, source_target_pairs={{1,0},{0,1},{3,2},{2,3},{5,4},{4,5},{7,6},{6,7},{9,8},{8,9},{11,10... | collective-permute-start | bytes 55304 | tf_op jit(solution)/shard_map/ppermute | solution.py:18
  4.1 50.5 %copy-start.9 = (f32[7,7,192]{2,1,0:T(8,128)}, f32[7,7,192]{2,1,0:T(8,128)S(1)}, u32[]{:S(2)}) copy-start(f32[7,7,192]{2,1,0:T(8,128)S(1)} %get-tuple-element.153) | copy-start | bytes 112900
  4.1 23.5 %copy-start.12 = (f32[1,1,192]{2,1,0:T(1,128)}, f32[1,1,192]{2,1,0:T(1,128)S(1)}, u32[]{:S(2)}) copy-start(f32[1,1,192]{2,1,0:T(1,128)S(1)} %get-tuple-element.113) | copy-start | bytes 2308
  4.1 23.5 %copy-start.14 = (f32[1,1,192]{2,1,0:T(1,128)}, f32[1,1,192]{2,1,0:T(1,128)S(1)}, u32[]{:S(2)}) copy-start(f32[1,1,192]{2,1,0:T(1,128)S(1)} %get-tuple-element.114) | copy-start | bytes 2308
  4.1 23.5 %copy-start.16 = (f32[1,1,192]{2,1,0:T(1,128)}, f32[1,1,192]{2,1,0:T(1,128)S(1)}, u32[]{:S(2)}) copy-start(f32[1,1,192]{2,1,0:T(1,128)S(1)} %get-tuple-element.115) | copy-start | bytes 2308
  4.1 23.5 %copy-start.18 = (f32[1,1,192]{2,1,0:T(1,128)}, f32[1,1,192]{2,1,0:T(1,128)S(1)}, u32[]{:S(2)}) copy-start(f32[1,1,192]{2,1,0:T(1,128)S(1)} %get-tuple-element.116) | copy-start | bytes 2308
  4.1 23.5 %copy-start.20 = (f32[1,1,192]{2,1,0:T(1,128)}, f32[1,1,192]{2,1,0:T(1,128)S(1)}, u32[]{:S(2)}) copy-start(f32[1,1,192]{2,1,0:T(1,128)S(1)} %get-tuple-element.117) | copy-start | bytes 2308
  4.1 23.5 %copy-start.22 = (f32[1,1,192]{2,1,0:T(1,128)}, f32[1,1,192]{2,1,0:T(1,128)S(1)}, u32[]{:S(2)}) copy-start(f32[1,1,192]{2,1,0:T(1,128)S(1)} %get-tuple-element.118) | copy-start | bytes 2308
  4.1 23.5 %copy-start.24 = (f32[1,1,192]{2,1,0:T(1,128)}, f32[1,1,192]{2,1,0:T(1,128)S(1)}, u32[]{:S(2)}) copy-start(f32[1,1,192]{2,1,0:T(1,128)S(1)} %get-tuple-element.119) | copy-start | bytes 2308
  7.7 17.6 %collective-permute-start.2 = (bf16[3,134,192]{1,2,0:T(8,128)(2,1)S(1)}, bf16[3,134,192]{1,2,0:T(8,128)(2,1)S(1)}, u32[]{:S(2)}, u32[]{:S(2)}) collective-permute-start(bf16[3,134,192]{1,2,0:T(8,128)(2,1)S(1)} %get-tuple-element.33), channel_id=1, source_target_pairs={{0,2},{2,4},{4,6},{6,8},{8,10},{10,12},{12,14},{1,3},{3,5},{5,7},{... | collective-permute-start | bytes 463112 | tf_op jit(solution)/shard_map/ppermute | solution.py:17
  12.6 12.7 %collective-permute-start.3 = (bf16[3,134,192]{1,2,0:T(8,128)(2,1)S(1)}, bf16[3,134,192]{1,2,0:T(8,128)(2,1)S(1)}, u32[]{:S(2)}, u32[]{:S(2)}) collective-permute-start(bf16[3,134,192]{1,2,0:T(8,128)(2,1)S(1)} %get-tuple-element.34), channel_id=1, source_target_pairs={{2,0},{4,2},{6,4},{8,6},{10,8},{12,10},{14,12},{3,1},{5,3},{7,5},{... | collective-permute-start | bytes 463112 | tf_op jit(solution)/shard_map/ppermute | solution.py:18
  53.5 1.7 collective-permute-start.4
  54.0 1.7 collective-permute-start.5
  56.4 17.2 %collective-permute-start.6 = (bf16[3,134,192]{1,2,0:T(8,128)(2,1)S(1)}, bf16[3,134,192]{1,2,0:T(8,128)(2,1)S(1)}, u32[]{:S(2)}, u32[]{:S(2)}) collective-permute-start(bf16[3,134,192]{1,2,0:T(8,128)(2,1)S(1)} %get-tuple-element.29), channel_id=1, source_target_pairs={{0,2},{2,4},{4,6},{6,8},{8,10},{10,12},{12,14},{1,3},{3,5},{5,7},{... | collective-permute-start | bytes 463112 | tf_op jit(solution)/shard_map/ppermute | solution.py:17
  60.9 12.8 %collective-permute-start.7 = (bf16[3,134,192]{1,2,0:T(8,128)(2,1)S(1)}, bf16[3,134,192]{1,2,0:T(8,128)(2,1)S(1)}, u32[]{:S(2)}, u32[]{:S(2)}) collective-permute-start(bf16[3,134,192]{1,2,0:T(8,128)(2,1)S(1)} %get-tuple-element.30), channel_id=1, source_target_pairs={{2,0},{4,2},{6,4},{8,6},{10,8},{12,10},{14,12},{3,1},{5,3},{7,5},{... | collective-permute-start | bytes 463112 | tf_op jit(solution)/shard_map/ppermute | solution.py:18
  108.4 1.3 collective-permute-start.8
  108.8 1.4 collective-permute-start.9
  111.0 11.9 %collective-permute-start.10 = (bf16[3,134,192]{1,2,0:T(8,128)(2,1)S(1)}, bf16[3,134,192]{1,2,0:T(8,128)(2,1)S(1)}, u32[]{:S(2)}, u32[]{:S(2)}) collective-permute-start(bf16[3,134,192]{1,2,0:T(8,128)(2,1)S(1)} %get-tuple-element.25), channel_id=1, source_target_pairs={{2,0},{4,2},{6,4},{8,6},{10,8},{12,10},{14,12},{3,1},{5,3},{7,5},{... | collective-permute-start | bytes 463112 | tf_op jit(solution)/shard_map/ppermute | solution.py:18
  112.7 17.4 %collective-permute-start.11 = (bf16[3,134,192]{1,2,0:T(8,128)(2,1)S(1)}, bf16[3,134,192]{1,2,0:T(8,128)(2,1)S(1)}, u32[]{:S(2)}, u32[]{:S(2)}) collective-permute-start(bf16[3,134,192]{1,2,0:T(8,128)(2,1)S(1)} %get-tuple-element.26), channel_id=1, source_target_pairs={{0,2},{2,4},{4,6},{6,8},{8,10},{10,12},{12,14},{1,3},{3,5},{5,7},{... | collective-permute-start | bytes 463112 | tf_op jit(solution)/shard_map/ppermute | solution.py:17
  158.5 1.3 collective-permute-start.12
  158.9 1.4 collective-permute-start.13
  161.1 11.9 %collective-permute-start.14 = (bf16[3,134,192]{1,2,0:T(8,128)(2,1)S(1)}, bf16[3,134,192]{1,2,0:T(8,128)(2,1)S(1)}, u32[]{:S(2)}, u32[]{:S(2)}) collective-permute-start(bf16[3,134,192]{1,2,0:T(8,128)(2,1)S(1)} %get-tuple-element.21), channel_id=1, source_target_pairs={{2,0},{4,2},{6,4},{8,6},{10,8},{12,10},{14,12},{3,1},{5,3},{7,5},{... | collective-permute-start | bytes 463112 | tf_op jit(solution)/shard_map/ppermute | solution.py:18
  162.4 17.1 %collective-permute-start.15 = (bf16[3,134,192]{1,2,0:T(8,128)(2,1)S(1)}, bf16[3,134,192]{1,2,0:T(8,128)(2,1)S(1)}, u32[]{:S(2)}, u32[]{:S(2)}) collective-permute-start(bf16[3,134,192]{1,2,0:T(8,128)(2,1)S(1)} %get-tuple-element.22), channel_id=1, source_target_pairs={{0,2},{2,4},{4,6},{6,8},{8,10},{10,12},{12,14},{1,3},{3,5},{5,7},{... | collective-permute-start | bytes 463112 | tf_op jit(solution)/shard_map/ppermute | solution.py:17
  (163 other events, 2574.7 us)
where the time goes:
time: 239 us; the launch traced here: 238 us
  other arithmetic  91.1 us (38%)
  waiting for transfers between devices  42.6 us (18%)
  blocking collectives  32.1 us (13%)
  starting transfers between devices  27.8 us (12%)
  matrix products  24.1 us (10%)
  local copies, waits for them, and re-layouts  13.4 us (6%)
  between operations  7.26 us (3%)
    reduce_sum x2, other arithmetic, project(): jnp.mean(values, axis=-1, keepdims=True)  36.4 us
    ppermute x8, waiting for transfers between devices, extended(): before = lax.ppermute(last, axis, up)  33.8 us
    psum x1, blocking collectives, on_device(): lax.psum((start_local, forward_local, adjoint_local), ('lat', 'lon'))  32.1 us
    ppermute x8, starting transfers between devices, extended(): before = lax.ppermute(last, axis, up)  20.7 us
    reduce_sum x1, other arithmetic, on_device(): start_local = jnp.sum(area_w * perturb * perturb)  18.2 us
    add x1, other arithmetic, on_device(): grad_field = grad_field + conv_back  17.1 us
    dot_general x2, matrix products, on_device(): lax.dot_general(gated, w_in[layer_index], (((2,), (1,)), ((), ())), prefe...  12.2 us
    dot_general x2, matrix products, on_device(): jnp.dot(gated, w_out[layer_index], preferred_element_type=jnp.float32)  11.9 us
  transfers between devices with their start and end apart: 16, of which 10 were waited for; matrix products, arithmetic and copies ran while one was open for 4% of the time, Pallas kernels for 0%

commit v1 on v0

--- a/solution.py
+++ b/solution.py
@@ -5,6 +5,12 @@
 from jax.sharding import PartitionSpec as P
 
 lat_span = 70.0 * math.pi / 180.0
+
+
+def check_strips_all(page, dev_axis, lane_axis):
+    for no in (dev_axis, lane_axis):
+        page = jax.lax.psum(page, no)
+    return page
 
 
 def extended(x, sides, width, wrap):
@@ -94,8 +100,8 @@
         grad_field = grad_field + conv_back
     adjoint_out = grad_field / area_w
     adjoint_local = jnp.sum(area_w * adjoint_out * adjoint_out)
-    start_sum, forward_sum, adjoint_sum = lax.psum(
-        (start_local, forward_local, adjoint_local), ("lat", "lon")
+    start_sum, forward_sum, adjoint_sum = check_strips_all(
+        (start_local, forward_local, adjoint_local), "lon", "lat"
     )
     start_sq = start_sum / weight_total
     forward_sq = forward_sum / weight_total

time: 239 us -> 231 us (0.967)
  blocking collectives: 32.1 us -> 23.8 us
    psum x1 -> x2, blocking collectives: 32.1 us -> 23.8 us  [check_strips_all(): page = jax.lax.psum(page, no)]
where the time goes in v1:
time: 231 us; the launch traced here: 230 us
  other arithmetic  91.2 us (39%)
  waiting for transfers between devices  42.4 us (18%)
  starting transfers between devices  27.8 us (12%)
  matrix products  24.1 us (10%)
  blocking collectives  23.8 us (10%)
  local copies, waits for them, and re-layouts  13.4 us (6%)
  between operations  7.33 us (3%)
    reduce_sum x2, other arithmetic, project(): jnp.mean(values, axis=-1, keepdims=True)  36.3 us
    ppermute x8, waiting for transfers between devices, extended(): before = lax.ppermute(last, axis, up)  33.8 us
    psum x2, blocking collectives, check_strips_all(): page = jax.lax.psum(page, no)  23.8 us
    ppermute x8, starting transfers between devices, extended(): before = lax.ppermute(last, axis, up)  20.7 us
    reduce_sum x1, other arithmetic, on_device(): start_local = jnp.sum(area_w * perturb * perturb)  18.2 us
    add x1, other arithmetic, on_device(): grad_field = grad_field + conv_back  17.1 us
    dot_general x2, matrix products, on_device(): lax.dot_general(gated, w_in[layer_index], (((2,), (1,)), ((), ())), prefe...  12.2 us
    dot_general x2, matrix products, on_device(): jnp.dot(gated, w_out[layer_index], preferred_element_type=jnp.float32)  11.9 us
  transfers between devices with their start and end apart: 16, of which 10 were waited for; matrix products, arithmetic and copies ran while one was open for 4% of the time, Pallas kernels for 0%

profile of v1, /device:TPU:0, one launch (start us, length us, event | category | flops | bytes accessed | tf_op | source)
XLA Modules:
  0.0 230.0 jit_solution(1334064928215537087)
XLA Ops:
  7.7 4.9 %collective-permute-start.2 = (bf16[3,134,192]{1,2,0:T(8,128)(2,1)S(1)}, bf16[3,134,192]{1,2,0:T(8,128)(2,1)S(1)}, u32[]{:S(2)}, u32[]{:S(2)}) collective-permute-start(bf16[3,134,192]{1,2,0:T(8,128)(2,1)S(1)} %get-tuple-element.36), channel_id=1, source_target_pairs={{0,2},{2,4},{4,6},{6,8},{8,10},{10,12},{12,14},{1,3},{3,5},{5,7},{... | collective-permute-start | bytes 463112 | tf_op jit(solution)/shard_map/ppermute | solution.py:23
  14.5 10.8 %collective-permute-done.2 = bf16[3,134,192]{1,2,0:T(8,128)(2,1)S(1)} collective-permute-done((bf16[3,134,192]{1,2,0:T(8,128)(2,1)S(1)}, bf16[3,134,192]{1,2,0:T(8,128)(2,1)S(1)}, u32[]{:S(2)}, u32[]{:S(2)}) %collective-permute-start.2) | collective-permute-done | bytes 154400 | tf_op jit(solution)/shard_map/ppermute | solution.py:23
  25.3 2.2 maximum_maximum_fusion
  28.0 18.3 %fusion.139 = (f32[16,128]{1,0:T(8,128)S(1)}, f32[16,128]{1,0:T(8,128)S(1)}, f32[16,128,192]{1,2,0:T(8,128)}) fusion(bf16[2,16,128,192]{2,3,1,0:T(8,128)(2,1)S(1)} %copy-done.5, bf16[19,134,192]{1,2,0:T(8,128)(2,1)S(1)} %get-tuple-element.35, f32[192]{0:T(256)S(1)} %bitcast.247, f32[192]{0:T(256)S(1)} %bitcast.249, f32[192]{0:T(256)S(1)} %bitcast.251, ...), kind=kLoop, calls=%fused_computation.193 | loop fusion | flops 66056192 | bytes 36266752 | tf_op jit(solution)/shard_map/reduce_sum | solution.py:56
  46.3 6.5 %fusion.153 = (bf16[16,128,192]{1,2,0:T(8,128)(2,1)S(1)}, f32[16,128,192]{1,2,0:T(8,128)}) fusion(f32[16,128,192]{1,2,0:T(8,128)} %param.9, bf16[2,768,192]{1,2,0:T(8,128)(2,1)S(1)} %copy-done.170, bf16[2,16,128,768]{3,2,1,0:T(8,128)(2,1)} %param.17, f32[16,128,192]{1,2,0:T(8,128)} %get-tuple-element.21, f32[16,128]{1,0:T(8,128)S(1)} %broadcast_multiply_fusion.6, ...), kind=kOutput, calls=%fused_computation.207 | convolution fusion | flops 1216610304 | bytes 10053632 | tf_op jit(solution)/shard_map/dot_general | solution.py:81
  56.4 4.4 %collective-permute-start.6 = (bf16[3,134,192]{1,2,0:T(8,128)(2,1)S(1)}, bf16[3,134,192]{1,2,0:T(8,128)(2,1)S(1)}, u32[]{:S(2)}, u32[]{:S(2)}) collective-permute-start(bf16[3,134,192]{1,2,0:T(8,128)(2,1)S(1)} %get-tuple-element.32), channel_id=1, source_target_pairs={{0,2},{2,4},{4,6},{6,8},{8,10},{10,12},{12,14},{1,3},{3,5},{5,7},{... | collective-permute-start | bytes 463112 | tf_op jit(solution)/shard_map/ppermute | solution.py:23
  64.8 8.8 %collective-permute-done.6 = bf16[3,134,192]{1,2,0:T(8,128)(2,1)S(1)} collective-permute-done((bf16[3,134,192]{1,2,0:T(8,128)(2,1)S(1)}, bf16[3,134,192]{1,2,0:T(8,128)(2,1)S(1)}, u32[]{:S(2)}, u32[]{:S(2)}) %collective-permute-start.6) | collective-permute-done | bytes 154400 | tf_op jit(solution)/shard_map/ppermute | solution.py:23
  76.3 18.0 %fusion.138 = (f32[16,128]{1,0:T(8,128)S(1)}, f32[16,128]{1,0:T(8,128)S(1)}, f32[16,128,192]{1,2,0:T(8,128)}) fusion(bf16[2,16,128,192]{2,3,1,0:T(8,128)(2,1)S(1)} %copy-done.6, bf16[19,134,192]{1,2,0:T(8,128)(2,1)S(1)} %get-tuple-element.31, f32[192]{0:T(256)S(1)} %bitcast.285, f32[192]{0:T(256)S(1)} %bitcast.287, f32[192]{0:T(256)S(1)} %bitcast.289, ...), kind=kLoop, calls=%fused_computation.192 | loop fusion | flops 66056192 | bytes 36266752 | tf_op jit(solution)/shard_map/reduce_sum | solution.py:56
  94.4 5.4 %multiply_add_fusion.1 = f32[16,128,192]{1,2,0:T(8,128)S(1)} fusion(f32[16,128,192]{1,2,0:T(8,128)} %get-tuple-element.153, bf16[2,16,128,768]{3,2,1,0:T(8,128)(2,1)} %param.17, f32[16,128,192]{1,2,0:T(8,128)} %get-tuple-element.20, f32[16,128]{1,0:T(8,128)S(1)} %broadcast_multiply_fusion.4, f32[16,128]{1,0:T(8,128)S(1)} %broadcast_multiply_fusion.5, ...), kind=kOutput, calls=%fused_computation.101 | convolution fusion | flops 1216217088 | bytes 9267200 | tf_op jit(solution)/shard_map/dot_general | solution.py:81
  99.9 6.0 %fusion.137 = (f32[16,128]{1,0:T(8,128)S(1)}, f32[16,128]{1,0:T(8,128)S(1)}, f32[16,128,192]{1,2,0:T(8,128)}) fusion(bf16[2,16,128,192]{2,3,1,0:T(8,128)(2,1)S(1)} %copy-done.7, bf16[2,192,768]{2,1,0:T(8,128)(2,1)} %param.12, bf16[2,16,128,768]{3,2,1,0:T(8,128)(2,1)} %param.17, f32[16,128,192]{1,2,0:T(8,128)S(1)} %multiply_add_fusion.1, ...), kind=kOutput, calls=%fused_computation.191 | convolution fusion | flops 1215819776 | bytes 7685696 | tf_op jit(solution)/shard_map/dot_general | solution.py:92
  112.7 5.4 %collective-permute-start.11 = (bf16[3,134,192]{1,2,0:T(8,128)(2,1)S(1)}, bf16[3,134,192]{1,2,0:T(8,128)(2,1)S(1)}, u32[]{:S(2)}, u32[]{:S(2)}) collective-permute-start(bf16[3,134,192]{1,2,0:T(8,128)(2,1)S(1)} %get-tuple-element.29), channel_id=1, source_target_pairs={{0,2},{2,4},{4,6},{6,8},{8,10},{10,12},{12,14},{1,3},{3,5},{5,7},{... | collective-permute-start | bytes 463112 | tf_op jit(solution)/shard_map/ppermute | solution.py:23
  118.1 4.8 %collective-permute-done.10 = bf16[3,134,192]{1,2,0:T(8,128)(2,1)S(1)} collective-permute-done((bf16[3,134,192]{1,2,0:T(8,128)(2,1)S(1)}, bf16[3,134,192]{1,2,0:T(8,128)(2,1)S(1)}, u32[]{:S(2)}, u32[]{:S(2)}) %collective-permute-start.10) | collective-permute-done | bytes 154400 | tf_op jit(solution)/shard_map/ppermute | solution.py:24
  122.9 7.2 %collective-permute-done.11 = bf16[3,134,192]{1,2,0:T(8,128)(2,1)S(1)} collective-permute-done((bf16[3,134,192]{1,2,0:T(8,128)(2,1)S(1)}, bf16[3,134,192]{1,2,0:T(8,128)(2,1)S(1)}, u32[]{:S(2)}, u32[]{:S(2)}) %collective-permute-start.11) | collective-permute-done | bytes 154400 | tf_op jit(solution)/shard_map/ppermute | solution.py:23
  130.1 2.2 pad_maximum_fusion.2
  132.7 17.1 %multiply_add_fusion = f32[16,128,192]{1,2,0:T(8,128)} fusion(f32[16,128,192]{1,2,0:T(8,128)S(1)} %copy-done.1, bf16[16,128,192]{1,2,0:T(8,128)(2,1)S(1)} %fusion.49, bf16[16,3,192]{1,2,0:T(8,128)(2,1)S(1)} %copy.29, bf16[16,3,192]{1,2,0:T(8,128)(2,1)S(1)} %copy.30, bf16[19,134,192]{1,2,0:T(8,128)(2,1)S(1)} %get-tuple-element.27, ...), kind=kLoop, calls=%fused_computation.35 | loop fusion | flops 65273856 | bytes 37036864 | tf_op jit(solution)/shard_map/add | solution.py:100
  149.8 6.2 %fusion.136 = (f32[16,128]{1,0:T(8,128)S(1)}, f32[16,128]{1,0:T(8,128)S(1)}, f32[16,128,192]{1,2,0:T(8,128)}) fusion(bf16[2,16,128,192]{2,3,1,0:T(8,128)(2,1)} %param.15, bf16[2,192,768]{2,1,0:T(8,128)(2,1)} %param.12, bf16[2,16,128,768]{3,2,1,0:T(8,128)(2,1)} %param.17, f32[16,128,192]{1,2,0:T(8,128)} %multiply_add_fusion, f32[192]{0:T(256)} %bitcast, ...), kind=kOutput, calls=%fused_computation.190 | convolution fusion | flops 1215426560 | bytes 7686144 | tf_op jit(solution)/shard_map/dot_general | solution.py:92
  162.4 5.3 %collective-permute-start.15 = (bf16[3,134,192]{1,2,0:T(8,128)(2,1)S(1)}, bf16[3,134,192]{1,2,0:T(8,128)(2,1)S(1)}, u32[]{:S(2)}, u32[]{:S(2)}) collective-permute-start(bf16[3,134,192]{1,2,0:T(8,128)(2,1)S(1)} %get-tuple-element.25), channel_id=1, source_target_pairs={{0,2},{2,4},{4,6},{6,8},{8,10},{10,12},{12,14},{1,3},{3,5},{5,7},{... | collective-permute-start | bytes 463112 | tf_op jit(solution)/shard_map/ppermute | solution.py:23
  169.5 3.5 %collective-permute-done.14 = bf16[3,134,192]{1,2,0:T(8,128)(2,1)S(1)} collective-permute-done((bf16[3,134,192]{1,2,0:T(8,128)(2,1)S(1)}, bf16[3,134,192]{1,2,0:T(8,128)(2,1)S(1)}, u32[]{:S(2)}, u32[]{:S(2)}) %collective-permute-start.14) | collective-permute-done | bytes 154400 | tf_op jit(solution)/shard_map/ppermute | solution.py:24
  173.0 6.5 %collective-permute-done.15 = bf16[3,134,192]{1,2,0:T(8,128)(2,1)S(1)} collective-permute-done((bf16[3,134,192]{1,2,0:T(8,128)(2,1)S(1)}, bf16[3,134,192]{1,2,0:T(8,128)(2,1)S(1)}, u32[]{:S(2)}, u32[]{:S(2)}) %collective-permute-start.15) | collective-permute-done | bytes 154400 | tf_op jit(solution)/shard_map/ppermute | solution.py:23
  179.5 2.2 pad_maximum_fusion.3
  182.1 18.2 %fusion.31 = (f32[]{:T(128)}, f32[]{:T(128)}, f32[]{:T(128)}, f32[16,128,192]{1,2,0:T(8,128)}) fusion(f32[16,128,192]{1,2,0:T(8,128)S(1)} %copy-done.4, f32[16]{0:T(128)} %multiply_cosine_fusion, f32[16,128,192]{1,2,0:T(8,128)S(1)} %copy-done.2, f32[16,128,192]{1,2,0:T(8,128)S(1)} %copy-done.3, bf16[19,134,192]{1,2,0:T(8,128)(2,1)S(1)} %get-tuple-element.23, ...), kind=kLoop, calls=%fused_computation.80 | loop fusion | flops 68812800 | bytes 40182604 | tf_op jit(solution)/shard_map/reduce_sum | solution.py:83
  200.4 3.1 %all-reduce.1 = (f32[]{:T(128)}, f32[]{:T(128)}, f32[]{:T(128)}) all-reduce(f32[]{:T(128)} %get-tuple-element.11, f32[]{:T(128)} %get-tuple-element.12, f32[]{:T(128)} %get-tuple-element.10), channel_id=1, replica_groups=mesh['grp'=2,'lat'=8,'lon'=2] {'lon'}, use_global_device_ids=true, to_apply=%region_9.0 | all-reduce | flops 3 | bytes 24 | tf_op jit(solution)/shard_map/psum | solution.py:12
  203.5 20.6 %all-reduce = (f32[]{:T(128)}, f32[]{:T(128)}, f32[]{:T(128)}) all-reduce(f32[]{:T(128)} %get-tuple-element.16, f32[]{:T(128)} %get-tuple-element.17, f32[]{:T(128)} %get-tuple-element.18), channel_id=1, replica_groups=mesh['grp'=2,'lat'=8,'lon'=2] {'lat'}, use_global_device_ids=true, to_apply=%region_10.0 | all-reduce | flops 3 | bytes 24 | tf_op jit(solution)/shard_map/psum | solution.py:12
  226.1 2.8 %broadcast_divide_fusion = f32[16,128,192]{1,2,0:T(8,128)} fusion(f32[16,128,192]{1,2,0:T(8,128)} %get-tuple-element.19, f32[16]{0:T(128)S(1)} %broadcast_multiply_fusion.8), kind=kLoop, calls=%fused_computation.133 | loop fusion | flops 393216 | bytes 3145792 | tf_op jit(solution)/shard_map/div | solution.py:110
  (414 shorter events, 32.2 us)
Async XLA Ops:
  2.9 3.5 %collective-permute-start = (bf16[16,3,192]{2,0,1:T(8,128)(2,1)S(1)}, bf16[16,3,192]{2,0,1:T(8,128)(2,1)S(1)}, u32[]{:S(2)}, u32[]{:S(2)}) collective-permute-start(bf16[16,3,192]{2,0,1:T(8,128)(2,1)S(1)} %copy.14), channel_id=1, source_target_pairs={{0,1},{1,0},{2,3},{3,2},{4,5},{5,4},{6,7},{7,6},{8,9},{9,8},{10,11... | collective-permute-start | bytes 55304 | tf_op jit(solution)/shard_map/ppermute | solution.py:23
  3.8 3.0 %collective-permute-start.1 = (bf16[16,3,192]{2,0,1:T(8,128)(2,1)S(1)}, bf16[16,3,192]{2,0,1:T(8,128)(2,1)S(1)}, u32[]{:S(2)}, u32[]{:S(2)}) collective-permute-start(bf16[16,3,192]{2,0,1:T(8,128)(2,1)S(1)} %copy.15), channel_id=1, source_target_pairs={{1,0},{0,1},{3,2},{2,3},{5,4},{4,5},{7,6},{6,7},{9,8},{8,9},{11,10... | collective-permute-start | bytes 55304 | tf_op jit(solution)/shard_map/ppermute | solution.py:24
  4.1 50.5 %copy-start.9 = (f32[7,7,192]{2,1,0:T(8,128)}, f32[7,7,192]{2,1,0:T(8,128)S(1)}, u32[]{:S(2)}) copy-start(f32[7,7,192]{2,1,0:T(8,128)S(1)} %get-tuple-element.156) | copy-start | bytes 112900
  4.1 23.5 %copy-start.12 = (f32[1,1,192]{2,1,0:T(1,128)}, f32[1,1,192]{2,1,0:T(1,128)S(1)}, u32[]{:S(2)}) copy-start(f32[1,1,192]{2,1,0:T(1,128)S(1)} %get-tuple-element.116) | copy-start | bytes 2308
  4.1 23.5 %copy-start.14 = (f32[1,1,192]{2,1,0:T(1,128)}, f32[1,1,192]{2,1,0:T(1,128)S(1)}, u32[]{:S(2)}) copy-start(f32[1,1,192]{2,1,0:T(1,128)S(1)} %get-tuple-element.117) | copy-start | bytes 2308
  4.1 23.5 %copy-start.16 = (f32[1,1,192]{2,1,0:T(1,128)}, f32[1,1,192]{2,1,0:T(1,128)S(1)}, u32[]{:S(2)}) copy-start(f32[1,1,192]{2,1,0:T(1,128)S(1)} %get-tuple-element.118) | copy-start | bytes 2308
  4.1 23.5 %copy-start.18 = (f32[1,1,192]{2,1,0:T(1,128)}, f32[1,1,192]{2,1,0:T(1,128)S(1)}, u32[]{:S(2)}) copy-start(f32[1,1,192]{2,1,0:T(1,128)S(1)} %get-tuple-element.119) | copy-start | bytes 2308
  4.1 23.5 %copy-start.20 = (f32[1,1,192]{2,1,0:T(1,128)}, f32[1,1,192]{2,1,0:T(1,128)S(1)}, u32[]{:S(2)}) copy-start(f32[1,1,192]{2,1,0:T(1,128)S(1)} %get-tuple-element.120) | copy-start | bytes 2308
  4.1 23.5 %copy-start.22 = (f32[1,1,192]{2,1,0:T(1,128)}, f32[1,1,192]{2,1,0:T(1,128)S(1)}, u32[]{:S(2)}) copy-start(f32[1,1,192]{2,1,0:T(1,128)S(1)} %get-tuple-element.121) | copy-start | bytes 2308
  4.1 23.5 %copy-start.24 = (f32[1,1,192]{2,1,0:T(1,128)}, f32[1,1,192]{2,1,0:T(1,128)S(1)}, u32[]{:S(2)}) copy-start(f32[1,1,192]{2,1,0:T(1,128)S(1)} %get-tuple-element.122) | copy-start | bytes 2308
  7.7 17.6 %collective-permute-start.2 = (bf16[3,134,192]{1,2,0:T(8,128)(2,1)S(1)}, bf16[3,134,192]{1,2,0:T(8,128)(2,1)S(1)}, u32[]{:S(2)}, u32[]{:S(2)}) collective-permute-start(bf16[3,134,192]{1,2,0:T(8,128)(2,1)S(1)} %get-tuple-element.36), channel_id=1, source_target_pairs={{0,2},{2,4},{4,6},{6,8},{8,10},{10,12},{12,14},{1,3},{3,5},{5,7},{... | collective-permute-start | bytes 463112 | tf_op jit(solution)/shard_map/ppermute | solution.py:23
  12.6 12.7 %collective-permute-start.3 = (bf16[3,134,192]{1,2,0:T(8,128)(2,1)S(1)}, bf16[3,134,192]{1,2,0:T(8,128)(2,1)S(1)}, u32[]{:S(2)}, u32[]{:S(2)}) collective-permute-start(bf16[3,134,192]{1,2,0:T(8,128)(2,1)S(1)} %get-tuple-element.37), channel_id=1, source_target_pairs={{2,0},{4,2},{6,4},{8,6},{10,8},{12,10},{14,12},{3,1},{5,3},{7,5},{... | collective-permute-start | bytes 463112 | tf_op jit(solution)/shard_map/ppermute | solution.py:24
  53.5 1.7 collective-permute-start.4
  54.0 1.7 collective-permute-start.5
  56.4 17.2 %collective-permute-start.6 = (bf16[3,134,192]{1,2,0:T(8,128)(2,1)S(1)}, bf16[3,134,192]{1,2,0:T(8,128)(2,1)S(1)}, u32[]{:S(2)}, u32[]{:S(2)}) collective-permute-start(bf16[3,134,192]{1,2,0:T(8,128)(2,1)S(1)} %get-tuple-element.32), channel_id=1, source_target_pairs={{0,2},{2,4},{4,6},{6,8},{8,10},{10,12},{12,14},{1,3},{3,5},{5,7},{... | collective-permute-start | bytes 463112 | tf_op jit(solution)/shard_map/ppermute | solution.py:23
  60.9 12.8 %collective-permute-start.7 = (bf16[3,134,192]{1,2,0:T(8,128)(2,1)S(1)}, bf16[3,134,192]{1,2,0:T(8,128)(2,1)S(1)}, u32[]{:S(2)}, u32[]{:S(2)}) collective-permute-start(bf16[3,134,192]{1,2,0:T(8,128)(2,1)S(1)} %get-tuple-element.33), channel_id=1, source_target_pairs={{2,0},{4,2},{6,4},{8,6},{10,8},{12,10},{14,12},{3,1},{5,3},{7,5},{... | collective-permute-start | bytes 463112 | tf_op jit(solution)/shard_map/ppermute | solution.py:24
  108.4 1.3 collective-permute-start.8
  108.8 1.4 collective-permute-start.9
  111.0 11.9 %collective-permute-start.10 = (bf16[3,134,192]{1,2,0:T(8,128)(2,1)S(1)}, bf16[3,134,192]{1,2,0:T(8,128)(2,1)S(1)}, u32[]{:S(2)}, u32[]{:S(2)}) collective-permute-start(bf16[3,134,192]{1,2,0:T(8,128)(2,1)S(1)} %get-tuple-element.28), channel_id=1, source_target_pairs={{2,0},{4,2},{6,4},{8,6},{10,8},{12,10},{14,12},{3,1},{5,3},{7,5},{... | collective-permute-start | bytes 463112 | tf_op jit(solution)/shard_map/ppermute | solution.py:24
  112.7 17.4 %collective-permute-start.11 = (bf16[3,134,192]{1,2,0:T(8,128)(2,1)S(1)}, bf16[3,134,192]{1,2,0:T(8,128)(2,1)S(1)}, u32[]{:S(2)}, u32[]{:S(2)}) collective-permute-start(bf16[3,134,192]{1,2,0:T(8,128)(2,1)S(1)} %get-tuple-element.29), channel_id=1, source_target_pairs={{0,2},{2,4},{4,6},{6,8},{8,10},{10,12},{12,14},{1,3},{3,5},{5,7},{... | collective-permute-start | bytes 463112 | tf_op jit(solution)/shard_map/ppermute | solution.py:23
  158.5 1.3 collective-permute-start.12
  158.9 1.4 collective-permute-start.13
  161.1 11.9 %collective-permute-start.14 = (bf16[3,134,192]{1,2,0:T(8,128)(2,1)S(1)}, bf16[3,134,192]{1,2,0:T(8,128)(2,1)S(1)}, u32[]{:S(2)}, u32[]{:S(2)}) collective-permute-start(bf16[3,134,192]{1,2,0:T(8,128)(2,1)S(1)} %get-tuple-element.24), channel_id=1, source_target_pairs={{2,0},{4,2},{6,4},{8,6},{10,8},{12,10},{14,12},{3,1},{5,3},{7,5},{... | collective-permute-start | bytes 463112 | tf_op jit(solution)/shard_map/ppermute | solution.py:24
  162.4 17.1 %collective-permute-start.15 = (bf16[3,134,192]{1,2,0:T(8,128)(2,1)S(1)}, bf16[3,134,192]{1,2,0:T(8,128)(2,1)S(1)}, u32[]{:S(2)}, u32[]{:S(2)}) collective-permute-start(bf16[3,134,192]{1,2,0:T(8,128)(2,1)S(1)} %get-tuple-element.25), channel_id=1, source_target_pairs={{0,2},{2,4},{4,6},{6,8},{8,10},{10,12},{12,14},{1,3},{3,5},{5,7},{... | collective-permute-start | bytes 463112 | tf_op jit(solution)/shard_map/ppermute | solution.py:23
  (163 other events, 2569.5 us)
